TPU v7x, 32 devices: a whole 2x2x4 slice. The times are simulated.
32 devices in a mesh: wide: 4 (over x, core), narrow: 8 (over z, y).
Axes of the slice: x: 2, y: 2, z: 4, core: 2. Of those that a mesh axis runs over, the one named last changes fastest.
Arguments:
- activations: bfloat16 [4, 32, 32, 1920], P(None, 'wide', None, 'narrow'), may hold values from -6 to 6
- covariance: float32 [17280, 17280], P('wide', 'narrow'), may hold values from -0.06 to 3, as said below
Outputs:
- updated: float32 [17280, 17280], P('wide', 'narrow')
Inputs may be any that keep to these rules, and one draw needn't show every extreme that they name: `covariance`: symmetric.
All inputs are finite; a program needn't handle non-finite values.
Results may differ from a plain program's by a relative error of at most 0.0003.
Values may be sent and summed in bfloat16 or wider, within the bound.
A program may use at most 384 MiB of HBM per device.

v0:
```python
import jax
import jax.numpy as jnp
from jax import lax
from jax.sharding import PartitionSpec as P

decay_rate = 0.9


def from_root(x, axis, root):
    mine = lax.axis_index(axis) == root
    return lax.psum(jnp.where(mine, x, jnp.zeros_like(x)), axis)


def extract_first(padded, rows_out, cols_out):
    tap_views = []
    for row_tap in range(3):
        for col_tap in range(3):
            tap_views.append(
                padded[:, :, row_tap : row_tap + rows_out, col_tap : col_tap + cols_out]
            )
    stacked = jnp.stack(tap_views, axis=1)
    shape = stacked.shape
    return stacked.reshape(shape[0] * shape[1], shape[2] * shape[3] * shape[4])


def pad_full(image):
    return jnp.pad(image, ((0, 0), (0, 0), (1, 1), (1, 1)))


def copy_slab(source, root):
    return from_root(source, "narrow", root)


def shards(activations, covariance):
    wide_count = lax.axis_size("wide")
    narrow_count = lax.axis_size("narrow")
    repeats = narrow_count // wide_count
    row_index = lax.axis_index("wide")
    width_cells = activations.shape[2]
    channels_first = jnp.transpose(activations, (3, 0, 1, 2))
    image = lax.all_gather(channels_first, "wide", axis=2, tiled=True)
    pieces = [copy_slab(image, row_index * repeats + offset) for offset in range(repeats)]
    row_image = jnp.concatenate(pieces, axis=0)
    full_rows = image.shape[2]
    column_patches = extract_first(pad_full(image), full_rows, width_cells)
    row_patches = extract_first(pad_full(row_image), full_rows, width_cells)
    product = lax.dot_general(
        row_patches, column_patches, (((1,), (1,)), ((), ())), preferred_element_type=jnp.float32
    )
    patch_count = column_patches.shape[1]
    return decay_rate * covariance + (1.0 - decay_rate) / patch_count * product


def solution(mesh):
    return jax.shard_map(
        shards,
        mesh=mesh,
        in_specs=(P(None, "wide", None, "narrow"), P("wide", "narrow")),
        out_specs=P("wide", "narrow"),
        check_vma=False,
    )
```

profile of v0, /device:TPU:0, one launch (start us, length us, event | category | flops | bytes accessed | tf_op | source)
XLA Modules:
  0.0 661.8 jit_solution(14366638017175099231)
XLA Ops:
  6.5 0.0 all-gather.2.cloned.1.call-start
  6.5 0.7 all-gather.2.cloned.1.call-update
  7.3 0.0 all-reduce.5.cloned.1.call-start
  7.3 26.9 %all-gather.2.cloned.1.call-done = bf16[240,4,32,32]{0,3,2,1:T(8,128)(2,1)} async-done(((bf16[240,4,8,32]{0,3,2,1:T(8,128)(2,1)}), bf16[240,4,32,32]{0,3,2,1:T(8,128)(2,1)}) %all-gather.2.cloned.1.call-update) | async-done | bytes 1966096 | tf_op jit(solution)/shard_map/all_gather | solution.py:41
  34.2 0.0 copy-start
  34.2 4.0 broadcast_select_fusion.1
  38.2 0.0 all-reduce.5.cloned.1.call-update
  38.2 0.0 copy-done
  38.2 2.1 fusion.18
  40.3 1.9 fusion.20
  42.2 2.5 fusion.22
  44.7 2.6 fusion.24
  47.3 1.5 bitcast_dynamic-update-slice_fusion.1
  48.8 2.6 fusion.26
  51.3 2.4 fusion.28
  53.7 1.8 fusion.30
  55.6 2.5 fusion.32
  58.1 74.4 %copy.4 = bf16[240,9,4,32,32]{4,3,2,1,0:T(8,128)(2,1)} copy(bf16[240,9,4,32,32]{0,4,3,2,1:T(8,128)(2,1)} %fusion.32) | data formatting | bytes 35389440 | tf_op jit(solution)/shard_map/stack | solution.py:21
  132.5 85.9 %reshape.7 = bf16[2160,4096]{1,0:T(8,128)(2,1)} reshape(bf16[240,9,4,32,32]{4,3,2,1,0:T(8,128)(2,1)} %copy.4) | data formatting | bytes 35389440 | tf_op jit(solution)/shard_map/reshape | solution.py:23
  218.4 0.0 all-reduce.5.cloned.1.call-done
  218.4 4.0 pad_maximum_fusion
  222.5 3.7 fusion.2
  226.2 3.0 fusion.4
  229.2 0.0 copy-start.1
  229.2 0.0 copy-start.2
  229.2 4.3 fusion.6
  233.5 4.5 fusion.8
  238.0 0.0 copy-done.1
  238.0 0.0 copy-done.2
  238.0 3.8 bitcast_dynamic-update-slice_fusion
  241.8 4.7 fusion.10
  246.6 4.3 fusion.12
  250.8 2.9 fusion.14
  253.8 4.4 fusion.16
  258.2 131.7 %copy.3 = bf16[480,9,4,32,32]{4,3,2,1,0:T(8,128)(2,1)} copy(bf16[480,9,4,32,32]{0,4,3,2,1:T(8,128)(2,1)} %fusion.16) | data formatting | bytes 70778880 | tf_op jit(solution)/shard_map/stack | solution.py:21
  389.9 169.8 %reshape.6 = bf16[4320,4096]{1,0:T(8,128)(2,1)} reshape(bf16[480,9,4,32,32]{4,3,2,1,0:T(8,128)(2,1)} %copy.3) | data formatting | bytes 70778880 | tf_op jit(solution)/shard_map/reshape | solution.py:23
  559.7 95.2 %fusion = f32[4320,2160]{1,0:T(8,128)} fusion(bf16[4320,4096]{1,0:T(8,128)(2,1)} %reshape.6, bf16[2160,4096]{1,0:T(8,128)(2,1)} %reshape.7, f32[4320,2160]{1,0:T(8,128)} %param.3), kind=kOutput, calls=%fused_computation.1 | convolution fusion | flops 76469182464 | bytes 127733760 | tf_op jit(solution)/shard_map/dot_general | solution.py:47
Async XLA Ops:
  6.5 27.7 %all-gather.2.cloned.1.call-start = ((), (), s32[]{:S(2)}) async-start(), calls=%async_computation | async-start | bytes 2621440 | tf_op jit(solution)/shard_map/all_gather | solution.py:41
  7.3 211.2 %all-reduce.5.cloned.1.call-start = ((), (), s32[]{:S(2)}) async-start(), calls=%async_computation.1 | async-start | bytes 8388608 | tf_op jit(solution)/shard_map/psum | solution.py:11
  34.2 4.0 copy-start
  229.2 8.8 %copy-start.1 = (bf16[240,4,32,32]{0,3,2,1:T(8,128)(2,1)S(1)}, bf16[240,4,32,32]{0,3,2,1:T(8,128)(2,1)}, u32[]{:S(2)}) copy-start(bf16[240,4,32,32]{0,3,2,1:T(8,128)(2,1)} %get-tuple-element.5) | copy-start | bytes 5898244
  229.2 8.8 %copy-start.2 = (bf16[240,4,32,32]{0,3,2,1:T(8,128)(2,1)S(1)}, bf16[240,4,32,32]{0,3,2,1:T(8,128)(2,1)}, u32[]{:S(2)}) copy-start(bf16[240,4,32,32]{0,3,2,1:T(8,128)(2,1)} %get-tuple-element.6) | copy-start | bytes 5898244
Sparse Core Ops, SparseCore 0:
  8.9 25.2 all-gather.1
  38.3 156.4 all-reduce.4
where the time goes:
time: 674 us; the launch traced here: 662 us
  local copies, waits for them, and re-layouts  514 us (76%)
  matrix products  95.2 us (14%)
  waiting for transfers between devices  27.6 us (4%)
  between operations  13.4 us (2%)
  other arithmetic  11.8 us (2%)
    reshape x2, local copies, waits for them, and re-layouts, extract_first(): return stacked.reshape(shape[0] * shape[1], shape[2] * shape[3] * shape[4])  256 us
    another operation x4, local copies, waits for them, and re-layouts, extract_first(): stacked = jnp.stack(tap_views, axis=1)  213 us
    dot_general x1, matrix products, shards(): lax.dot_general(row_patches, column_patches, (((1,), (1,)), ((), ())), pr...  95.2 us
    unnamed x21, local copies, waits for them, and re-layouts  44.8 us
    all_gather x1, waiting for transfers between devices, shards(): image = lax.all_gather(channels_first, 'wide', axis=2, tiled=True)  26.9 us
  transfers between devices with their start and end apart: 2, of which 1 were waited for; matrix products, arithmetic and copies ran while one was open for 27% of the time, Pallas kernels for 0%

commit v1 on v0

v1 whole, which is shorter than its diff:
```python
import functools

import jax
import jax.numpy as jnp
from jax import lax
from jax.experimental import pallas as pl
from jax.experimental.pallas import tpu as pltpu
from jax.sharding import PartitionSpec as P

decay_rate = 0.9


def expand_kernel(width, height, image_ref, out_ref, spread):
    group, positions = image_ref.shape
    image = image_ref[...].astype(jnp.float32)
    place = lax.broadcasted_iota(jnp.int32, (8, positions), 1)
    column = place % width
    row = (place // width) % height
    row_ok = [row >= 1, None, row < height - 1]
    column_ok = [column >= 1, None, column < width - 1]
    for a in range(3):
        for b in range(3):
            offset = (a - 1) * width + (b - 1)
            moved = pltpu.roll(image, (-offset) % positions, 1) if offset else image
            keep = row_ok[a]
            if column_ok[b] is not None:
                keep = column_ok[b] if keep is None else keep & column_ok[b]
            for half in range(group // 8):
                part = moved[half * 8 : half * 8 + 8]
                if keep is not None:
                    part = jnp.where(keep, part, 0.0)
                for tile in range(positions // 128):
                    spread[tile, pl.ds(half * 72 + 3 * a + b, 8, stride=9), :] = part[
                        :, tile * 128 : tile * 128 + 128
                    ]
    for tile in range(positions // 128):
        out_ref[:, tile * 128 : tile * 128 + 128] = spread[tile].astype(jnp.bfloat16)


def expand(image, width, height):
    channels, positions = image.shape
    group = 16 if channels % 16 == 0 else 8
    return pl.pallas_call(
        functools.partial(expand_kernel, width, height),
        grid=(channels // group,),
        out_shape=jax.ShapeDtypeStruct((channels * 9, positions), jnp.bfloat16),
        in_specs=[pl.BlockSpec((group, positions), lambda i: (i, 0))],
        out_specs=pl.BlockSpec((group * 9, positions), lambda i: (i, 0)),
        scratch_shapes=[pltpu.VMEM((positions // 128, group * 9, 128), jnp.float32)],
        cost_estimate=pl.CostEstimate(
            flops=channels * 9 * positions * 20,
            bytes_accessed=channels * positions * 20,
            transcendentals=0,
        ),
    )(image)


def update_kernel(width, height, new_share, image_ref, edge_ref, patches_ref, low_ref, side_ref, covariance_ref, *rest):
    out_ref, corners, gram, spread = rest[-4:]
    group, positions = image_ref.shape
    columns = covariance_ref.shape[1]
    tiles = -(-columns // 128)
    image = image_ref[...].astype(jnp.float32)
    place = lax.broadcasted_iota(jnp.int32, (1, positions), 1)
    column = place % width
    row = (place // width) % height
    row_ok = [row >= 1, None, row < height - 1]
    column_ok = [column >= 1, None, column < width - 1]
    planes = []
    for a, b in ((0, 0), (0, 2), (2, 0), (2, 2)):
        offset = (a - 1) * width + (b - 1)
        moved = pltpu.roll(image, (-offset) % positions, 1)
        planes.append(jnp.where(row_ok[a] & column_ok[b], moved, 0.0))
    corners[...] = jnp.concatenate(planes, axis=0).astype(jnp.bfloat16)
    contract = (((1,), (1,)), ((), ()))
    gram[0 : 4 * group, 128 : 128 + columns] = lax.dot_general(
        corners[...], patches_ref[...], contract, preferred_element_type=jnp.float32
    )
    size = low_ref.shape[1]
    edge = edge_ref[...].astype(jnp.float32)
    edge = [edge[:, k * size : k * size + size] for k in (0, 2, 3, 4, 5)]
    low = lax.dot_general(
        jnp.concatenate(edge[:2], axis=0).astype(jnp.bfloat16), low_ref[...], contract, preferred_element_type=jnp.float32
    )
    gram[4 * group : 6 * group, 128 : 128 + columns] = low
    side = lax.dot_general(
        jnp.concatenate(edge[2:], axis=0).astype(jnp.bfloat16), side_ref[...], contract, preferred_element_type=jnp.float32
    )
    gram[6 * group : 9 * group, 128 : 128 + columns] = side

    def shifted(plane, tile, by):
        near = gram[plane * group : plane * group + group, tile * 128 : tile * 128 + 384]
        return pltpu.roll(near, by % 384, 1)[:, 128:256]

    for tile in range(tiles):
        tap = (lax.broadcasted_iota(jnp.int32, (1, 128), 1) + tile * 128) % 9
        here = slice(128 + tile * 128, 256 + tile * 128)
        for b in range(2):
            mine = slice((4 + b) * group, (5 + b) * group)
            gram[mine, here] = gram[mine, here] + jnp.where(
                tap < 3, shifted(2 + b, tile, -3), shifted(b, tile, 3)
            )
    first = (0, 4, 2)
    for tile in range(tiles):
        lane = lax.broadcasted_iota(jnp.int32, (1, 128), 1) + tile * 128
        here = slice(128 + tile * 128, 256 + tile * 128)
        for a in range(3):
            left = first[a]
            middle = gram[(6 + a) * group : (7 + a) * group, here] + jnp.where(
                lane % 3 == 0, shifted(left + 1, tile, -1), shifted(left, tile, 1)
            )
            taps = (
                gram[left * group : (left + 1) * group, here],
                middle,
                gram[(left + 1) * group : (left + 2) * group, here],
            )
            for b in range(3):
                spread[tile, pl.ds(3 * a + b, group, stride=9), :] = taps[b]
        end = min(columns, tile * 128 + 128)
        cut = slice(tile * 128, end)
        out_ref[:, cut] = (
            decay_rate * covariance_ref[:, cut] + new_share * spread[tile][:, : end - tile * 128]
        )


def update(image, edges, patches, low, side, covariance, group, first, steps, slabs, so_far, width, height):
    channels, positions = image.shape
    columns = covariance.shape[1]
    each = covariance.shape[0] // (9 * group * slabs)
    padded = -(-columns // 128) * 128 + 256
    whole = lambda i: (0, 0)
    once = pl.Buffered(1)
    tile = pl.BlockSpec(
        (group * 9, columns), lambda i: ((i // steps) * each + first + i % steps, 0)
    )
    operands = [image, edges, patches, low, side, covariance]
    specs = [
        pl.BlockSpec((group, positions), lambda i: (i, 0)),
        pl.BlockSpec((group, edges.shape[1]), lambda i: (i, 0)),
        pl.BlockSpec(patches.shape, whole, pipeline_mode=once),
        pl.BlockSpec(low.shape, whole, pipeline_mode=once),
        pl.BlockSpec(side.shape, whole, pipeline_mode=once),
        tile,
    ]
    aliases = {}
    if so_far is not None:
        operands.append(so_far)
        specs.append(pl.BlockSpec(memory_space=pl.ANY))
        aliases = {6: 0}
    return pl.pallas_call(
        functools.partial(update_kernel, width, height, (1.0 - decay_rate) / positions),
        grid=(slabs * steps,),
        out_shape=jax.ShapeDtypeStruct(covariance.shape, jnp.float32),
        in_specs=specs,
        out_specs=tile,
        scratch_shapes=[
            pltpu.VMEM((4 * group, positions), jnp.bfloat16),
            pltpu.VMEM((9 * group, padded), jnp.float32),
            pltpu.VMEM((-(-columns // 128), group * 9, 128), jnp.float32),
        ],
        input_output_aliases=aliases,
        cost_estimate=pl.CostEstimate(
            flops=2 * 4 * channels * positions * columns,
            bytes_accessed=channels * 9 * columns * 8 + patches.size * 2,
            transcendentals=0,
        ),
        compiler_params=pltpu.CompilerParams(vmem_limit_bytes=62 * 1024 * 1024),
    )(*operands)


def edge_selector(batch, height, width):
    place = lax.broadcasted_iota(jnp.int32, (batch * height * width, 1), 0)
    parts = []
    for size, last, stride in ((width, (height - 1) * width, 1), (height, width - 1, width)):
        line = lax.broadcasted_iota(jnp.int32, (1, batch * size), 1)
        for k in (-1, 0, 1):
            at = line % size + k
            wanted = (line // size) * height * width + last + at * stride
            parts.append((place == wanted) & (at >= 0) & (at < size))
    return jnp.concatenate(parts, axis=1).astype(jnp.bfloat16)


def edge_values(image, selector):
    return lax.dot_general(
        image, selector, (((1,), (0,)), ((), ())), preferred_element_type=jnp.float32
    ).astype(jnp.bfloat16)


def interleave(planes):
    empty = jnp.zeros_like(next(iter(planes.values())))
    stacked = jnp.stack([planes.get(t, empty) for t in range(9)], axis=1)
    return stacked.reshape(-1, stacked.shape[2])


def shards(activations, covariance):
    wide_count = lax.axis_size("wide")
    narrow_count = lax.axis_size("narrow")
    repeats = narrow_count // wide_count
    batch, rows, width, channels = activations.shape
    height = rows * wide_count
    strip = jnp.transpose(activations.reshape(batch * rows * width, channels)).reshape(
        channels, batch, rows * width
    )
    moves = []
    for r in range(wide_count):
        for s in range(narrow_count):
            target = (s // repeats) * narrow_count + r + (s % repeats) * wide_count
            moves.append((r * narrow_count + s, target))
    row_strip = lax.ppermute(strip, ("wide", "narrow"), moves)
    group = max(g for g in range(8, 49, 8) if channels % g == 0)
    steps = channels // group
    cuts = [0, (steps * 2) // 5, steps] if steps > 3 else [0, steps]
    positions = batch * height * width
    column_strips = lax.all_gather(strip, "wide")
    row_parts = []
    for low_cut, high_cut in zip(cuts[:-1], cuts[1:]):
        piece = row_strip[low_cut * group : high_cut * group]
        if row_parts:
            piece, row_parts[-1] = lax.optimization_barrier((piece, row_parts[-1]))
        row_parts.append(lax.all_gather(piece, "narrow"))
    selector = edge_selector(batch, height, width)
    column_image = jnp.transpose(column_strips, (1, 2, 0, 3)).reshape(channels, positions)
    patches = expand(column_image, width, height)
    edges = edge_values(column_image, selector)
    size = edges.shape[1] // 6
    edge = [edges[:, k * size : k * size + size] for k in range(6)]
    low = interleave({3 + b: edge[b] for b in range(3)})
    side = interleave({3 * a + 1: edge[3 + a] for a in range(3)})
    updated = None
    for part, first in enumerate(cuts[:-1]):
        count = cuts[part + 1] - first
        own = count * group
        image = jnp.transpose(
            row_parts[part].reshape(repeats, wide_count, own, batch, rows * width), (0, 2, 3, 1, 4)
        ).reshape(repeats * own, positions)
        edges = edge_values(image, selector)
        updated = update(
            image, edges, patches, low, side, covariance, group, first, count, repeats, updated, width, height
        )
    return updated


def solution(mesh):
    return jax.shard_map(
        shards,
        mesh=mesh,
        in_specs=(P(None, "wide", None, "narrow"), P("wide", "narrow")),
        out_specs=P("wide", "narrow"),
        check_vma=False,
    )
```

time: 674 us -> 261 us (0.39); the launches traced: 662 us -> 261 us
  local copies, waits for them, and re-layouts: 514 us -> 30.2 us
  Pallas kernels: 0 us -> 101 us
  matrix products: 95.2 us -> 14.9 us
  waiting for transfers between devices: 27.6 us -> 92.9 us
    reshape x2 -> x7, local copies, waits for them, and re-layouts: 256 us -> 11.5 us  [the longest x2 4.15 us: shards(): image = jnp.transpose(row_parts[part].reshape(repeats, wide_count, own, b...]
    another operation x4 -> x13, local copies, waits for them, and re-layouts: 213 us -> 6.8 us  [the longest x9 5.47 us: interleave(): stacked = jnp.stack([planes.get(t, empty) for t in range(9)], axis=1)]
    pallas_call x0 -> x3, Pallas kernels: none -> 101 us  [the longest x2 85.8 us: update(): pl.pallas_call(functools.partial(update_kernel, width, height, (1.0 - dec...]
    dot_general x1 -> x3, matrix products: 95.2 us -> 14.9 us  [edge_values(): lax.dot_general(image, selector, (((1,), (0,)), ((), ())), preferred_elem...]
    all_gather x1 -> x3, waiting for transfers between devices: 26.9 us -> 92.8 us  [the longest x2 75.3 us: shards(): row_parts.append(lax.all_gather(piece, 'narrow'))]
    unnamed x21 -> x4, local copies, waits for them, and re-layouts: 44.8 us -> 0.01 us
    transpose x0 -> x3, local copies, waits for them, and re-layouts: none -> 6.77 us  [the longest x1 4.33 us: shards(): jnp.transpose(column_strips, (1, 2, 0, 3)).reshape(channels, positions)]
  transfers between devices with their start and end apart: 2 -> 4, of which waited for: 1 -> 2; matrix products, arithmetic and copies ran while one was open for 27% -> 15% of each run, Pallas kernels for 0% -> 20%
where the time goes in v1:
time: 261 us
  Pallas kernels  101 us (39%)
  waiting for transfers between devices  92.9 us (36%)
  local copies, waits for them, and re-layouts  30.2 us (12%)
  matrix products  14.9 us (6%)
  between operations  13.3 us (5%)
  other arithmetic  7.94 us (3%)
    pallas_call x2, Pallas kernels, update(): pl.pallas_call(functools.partial(update_kernel, width, height, (1.0 - dec...  85.8 us
    all_gather x2, waiting for transfers between devices, shards(): row_parts.append(lax.all_gather(piece, 'narrow'))  75.3 us
    all_gather x1, waiting for transfers between devices, shards(): column_strips = lax.all_gather(strip, 'wide')  17.5 us
    dot_general x3, matrix products, edge_values(): lax.dot_general(image, selector, (((1,), (0,)), ((), ())), preferred_elem...  14.9 us
    pallas_call x1, Pallas kernels, expand(): pl.pallas_call(functools.partial(expand_kernel, width, height), grid=(cha...  14.8 us
    unnamed x5, other arithmetic  6.59 us
    another operation x9, local copies, waits for them, and re-layouts, interleave(): stacked = jnp.stack([planes.get(t, empty) for t in range(9)], axis=1)  5.47 us
  transfers between devices with their start and end apart: 4, of which 2 were waited for; matrix products, arithmetic and copies ran while one was open for 15% of the time, Pallas kernels for 20%

profile of v1, /device:TPU:0, one launch (start us, length us, event | category | flops | bytes accessed | tf_op | source)
XLA Modules:
  0.0 260.7 jit_solution(13374366034493032529)
XLA Ops:
  6.5 0.0 all-gather.8.cloned.1.call-start
  6.5 1.2 copy.35
  7.8 0.4 reshape.130
  8.1 0.7 collective-permute-start
  8.8 0.0 collective-permute-done
  8.8 0.7 slice.33
  9.6 0.0 all-gather.8.cloned.1.call-update
  9.6 0.0 all-gather.6.cloned.1.call-start
  9.7 0.4 all_gather_reshape.3
  10.0 0.8 copy.39
  10.9 0.0 all-gather.6.cloned.1.call-update
  10.9 0.0 all-gather.10.cloned.1.call-start
  11.0 1.3 fusion.2
  12.4 1.3 fusion.5
  13.7 1.3 fusion.8
  15.0 1.3 fusion.11
  16.3 0.8 slice.32
  17.1 75.3 %all-gather.8.cloned.1.call-done = bf16[768,4,256]{2,1,0:T(4,128)(2,1)} async-done(((bf16[96,4,256]{2,1,0:T(4,128)(2,1)}), bf16[768,4,256]{2,1,0:T(4,128)(2,1)}) %all-gather.8.cloned.1.call-update) | async-done | bytes 1572880 | tf_op jit(solution)/shard_map/all_gather | solution.py:220
  92.4 1.6 copy.36
  94.1 0.0 all-gather.10.cloned.1.call-update
  94.1 1.3 fusion.14
  95.4 1.3 fusion.17
  96.7 17.5 %all-gather.6.cloned.1.call-done = bf16[4,240,4,256]{3,1,2,0:T(8,128)(2,1)} async-done(((bf16[1,240,4,256]{3,1,2,0:T(8,128)(2,1)}), bf16[4,240,4,256]{3,1,2,0:T(8,128)(2,1)}) %all-gather.6.cloned.1.call-update) | async-done | bytes 1966096 | tf_op jit(solution)/shard_map/all_gather | solution.py:214
  114.2 4.3 %copy.40 = bf16[240,4,4,256]{3,2,1,0:T(4,128)(2,1)} copy(bf16[240,4,4,256]{3,0,1,2:T(8,128)(2,1)} %bitcast.34) | data formatting | bytes 3932160 | tf_op jit(solution)/shard_map/transpose | solution.py:222
  118.6 3.5 %reshape.133.image_ref = bf16[240,4096]{1,0:T(8,128)(2,1)S(1)} reshape(bf16[240,4,4,256]{3,2,1,0:T(4,128)(2,1)} %copy.40) | data formatting | bytes 3932160 | tf_op jit(solution)/shard_map/reshape | solution.py:222
  122.1 0.0 copy-start
  122.1 4.4 %fusion.18 = bf16[240,768]{1,0:T(8,128)(2,1)S(1)} fusion(pred[4096,768]{1,0:T(8,128)(4,1)} %fusion.17, bf16[240,4096]{1,0:T(8,128)(2,1)S(1)} %reshape.133.image_ref), kind=kOutput, calls=%fused_computation.27 | convolution fusion | flops 1510133760 | bytes 5480448 | tf_op jit(solution)/shard_map/dot_general | solution.py:184
  126.5 0.0 copy-done
  126.5 0.1 slice_bitcast_fusion
  126.6 0.1 copy.46
  126.7 0.1 copy.45
  126.8 0.1 copy.44
  126.9 0.1 copy.43
  127.0 0.1 copy.42
  127.1 0.1 copy.41
  127.2 0.1 broadcast.428
  127.3 0.1 broadcast.427
  127.4 3.2 %stack.27 = bf16[240,9,128]{2,1,0:T(8,128)(2,1)S(1)} concatenate(bf16[240,1,128]{2,1,0:T(2,128)(2,1)S(1)} %broadcast.427, bf16[240,2,128]{2,1,0:T(2,128)(2,1)S(1)} %broadcast.428, bf16[240,1,128]{2,1,0:T(2,128)(2,1)S(1)} %copy.41, bf16[240,1,128]{2,1,0:T(2,128)(2,1)S(1)} %copy.42, bf16[240,1,128]{2,1,0:T(2,128)(2,1)S(1)} %copy.43, bf16[240,1,128]{2,1,0:T(2,128)(2,1)S(1)} %broadcast.427, ...), dimensions={1} | concatenate | bytes 1105920 | tf_op jit(solution)/shard_map/stack | solution.py:191
  130.6 1.1 reshape.134.low_ref
  131.8 1.6 stack.31
  133.3 1.1 reshape.135.side_ref
  134.5 14.8 %shard_map.28.patches_ref = bf16[2160,4096]{1,0:T(8,128)(2,1)} custom-call(bf16[240,4096]{1,0:T(8,128)(2,1)} %copy-done), custom_call_target="tpu_custom_call" | custom-call | flops 176947200 | bytes 19660800 | tf_op jit(solution)/shard_map/pallas_call | solution.py:43
  149.3 1.2 copy.48
  150.5 1.2 reshape.137.image_ref
  151.7 0.0 copy-start.1
  151.7 5.1 %convolution_convert_fusion.2.edge_ref = bf16[192,768]{1,0:T(8,128)(2,1)} fusion(bf16[192,4096]{1,0:T(8,128)(2,1)S(1)} %reshape.137.image_ref, pred[4096,768]{1,0:T(8,128)(4,1)} %fusion.17), kind=kOutput, calls=%fused_computation.26 | convolution fusion | flops 1208107008 | bytes 5013504 | tf_op jit(solution)/shard_map/dot_general | solution.py:184
  156.8 0.0 copy-done.1
  156.8 36.3 %shard_map.29.rest_0_ = f32[4320,2160]{1,0:T(8,128)} custom-call(bf16[192,4096]{1,0:T(8,128)(2,1)} %copy-done.1, bf16[192,768]{1,0:T(8,128)(2,1)} %convolution_convert_fusion.2.edge_ref, bf16[2160,4096]{1,0:T(8,128)(2,1)} %shard_map.28.patches_ref, bf16[2160,128]{1,0:T(8,128)(2,1)} %reshape.134.low_ref, bf16[2160,128]{1,0:T(8,128)(2,1)} %reshape.135.side_ref, ...), custom_call_target="tpu_custom_call" | custom-call | flops 13589544960 | bytes 47554560 | tf_op jit(solution)/shard_map/pallas_call | solution.py:150
  193.1 0.0 all-gather.10.cloned.1.call-done
  193.1 2.0 copy.37
  195.0 1.2 copy.38
  196.3 2.9 %reshape.132.image_ref = bf16[288,4096]{1,0:T(8,128)(2,1)} reshape(bf16[2,144,4,4,256]{4,3,2,1,0:T(4,128)(2,1)S(1)} %copy.38) | data formatting | bytes 4718592 | tf_op jit(solution)/shard_map/reshape | solution.py:235
  199.2 5.4 %convolution_convert_fusion.edge_ref = bf16[288,768]{1,0:T(8,128)(2,1)} fusion(bf16[288,4096]{1,0:T(8,128)(2,1)} %reshape.132.image_ref, pred[4096,768]{1,0:T(8,128)(4,1)} %fusion.17), kind=kOutput, calls=%fused_computation.24 | convolution fusion | flops 1812160512 | bytes 5947392 | tf_op jit(solution)/shard_map/dot_general | solution.py:184
  204.6 49.5 %shard_map.30 = f32[4320,2160]{1,0:T(8,128)} custom-call(bf16[288,4096]{1,0:T(8,128)(2,1)} %reshape.132.image_ref, bf16[288,768]{1,0:T(8,128)(2,1)} %convolution_convert_fusion.edge_ref, bf16[2160,4096]{1,0:T(8,128)(2,1)} %shard_map.28.patches_ref, bf16[2160,128]{1,0:T(8,128)(2,1)} %reshape.134.low_ref, ...), custom_call_target="tpu_custom_call", output_to_operand_aliasing={{}: (6, {})} | custom-call | flops 20384317440 | bytes 62484480 | tf_op jit(solution)/shard_map/pallas_call | solution.py:150
  (9 shorter events, 0.1 us)
Async XLA Ops:
  6.5 85.9 %all-gather.8.cloned.1.call-start = ((), (), s32[]{:S(2)}) async-start(), calls=%async_computation.1 | async-start | bytes 1769472 | tf_op jit(solution)/shard_map/all_gather | solution.py:220
  8.1 0.7 collective-permute-start
  9.6 104.6 %all-gather.6.cloned.1.call-start = ((), (), s32[]{:S(2)}) async-start(), calls=%async_computation | async-start | bytes 2457600 | tf_op jit(solution)/shard_map/all_gather | solution.py:214
  10.9 182.2 %all-gather.10.cloned.1.call-start = ((), (), s32[]{:S(2)}) async-start(), calls=%async_computation.2 | async-start | bytes 2654208 | tf_op jit(solution)/shard_map/all_gather | solution.py:220
  122.1 4.5 %copy-start = (bf16[240,4096]{1,0:T(8,128)(2,1)}, bf16[240,4096]{1,0:T(8,128)(2,1)S(1)}, u32[]{:S(2)}) copy-start(bf16[240,4096]{1,0:T(8,128)(2,1)S(1)} %reshape.133.image_ref) | copy-start | bytes 5898244
  151.7 5.1 %copy-start.1 = (bf16[192,4096]{1,0:T(8,128)(2,1)}, bf16[192,4096]{1,0:T(8,128)(2,1)S(1)}, u32[]{:S(2)}) copy-start(bf16[192,4096]{1,0:T(8,128)(2,1)S(1)} %reshape.137.image_ref) | copy-start | bytes 4718596
Sparse Core Ops, SparseCore 0:
  9.7 82.6 all-gather.7
  94.0 20.1 all-gather.5
  116.4 51.8 all-gather.9
